TPU v7x, 32 devices: a whole 2x2x4 slice. The times are simulated.
32 devices in a mesh: dp: 2 (over core), cent: 16 (over z, y, x).
Axes of the slice: x: 2, y: 2, z: 4, core: 2. Of those that a mesh axis runs over, the one named last changes fastest.
Arguments:
- embeddings: bfloat16 [4096, 768], P(('dp', 'cent')), may hold values from -20 to 20
- fine_centroids: float32 [8192, 768], P('cent'), may hold values from -8 to 8
- parents: int32 [8192], P('cent'), may hold values from 0 to 2047
- coarse_centroids: float32 [2048, 768], P('cent'), may hold values from -6 to 6
Outputs:
- new_fine: float32 [8192, 768], P('cent')
- new_coarse: float32 [2048, 768], P('cent')
All inputs are finite; a program needn't handle non-finite values.
Results may differ from a plain program's by a relative error of at most 0.004.
Values may be sent and summed in bfloat16 or wider, within the bound.
A program may use at most 64 MiB of HBM per device.

v0:
```python
import math
import jax
import jax.numpy as jnp
from jax import lax
from jax.sharding import PartitionSpec as P

KC = 2048
sharpness = 0.1
coarse_prior = 16.0


def block_logits(one_block, narrow_centroids, half_norm):
    scores = lax.dot_general(
        one_block, narrow_centroids, (((1,), (1,)), ((), ())), preferred_element_type=jnp.float32
    )
    return sharpness * (scores - half_norm[None, :])


def coarse_terms(parent_ids, pooled, mass_rows):
    summed = jax.ops.segment_sum(pooled, parent_ids, num_segments=KC)
    weighted = jax.ops.segment_sum(mass_rows, parent_ids, num_segments=KC)
    return (summed, weighted)


def local(embeddings, fine_centroids, parents, coarse_centroids):
    gathered = lax.all_gather(embeddings, "cent", axis=0, tiled=True)
    row_count = gathered.shape[0]
    feat_width = gathered.shape[1]
    block_rows = math.gcd(row_count, 512)
    row_blocks = gathered.reshape(row_count // block_rows, block_rows, feat_width)
    narrow_centroids = fine_centroids.astype(jnp.bfloat16)
    half_norm = 0.5 * jnp.sum(fine_centroids * fine_centroids, axis=1)
    no_carry = jnp.zeros((), jnp.float32)

    def peak_step(carried, one_block):
        logits = block_logits(one_block, narrow_centroids, half_norm)
        return (carried, jnp.max(logits, axis=1))

    _, local_peak = lax.scan(peak_step, no_carry, row_blocks)
    row_peak = lax.pmax(local_peak.reshape(-1), "cent")

    def mass_step(carried, items):
        one_block, block_peak = items
        logits = block_logits(one_block, narrow_centroids, half_norm)
        return (carried, jnp.sum(jnp.exp(logits - block_peak[:, None]), axis=1))

    _, local_mass = lax.scan(mass_step, no_carry, (row_blocks, row_peak.reshape(-1, block_rows)))
    row_mass = lax.psum(local_mass.reshape(-1), "cent")

    def sum_step(carried, items):
        one_block, block_peak, block_mass = items
        logits = block_logits(one_block, narrow_centroids, half_norm)
        soft_weights = jnp.exp(logits - block_peak[:, None]) / block_mass[:, None]
        wide_block = one_block.astype(jnp.float32)
        summed = carried[0] + lax.dot_general(
            soft_weights,
            wide_block,
            (((0,), (0,)), ((), ())),
            precision=lax.Precision.HIGHEST,
            preferred_element_type=jnp.float32,
        )
        counted = carried[1] + jnp.sum(soft_weights, axis=0)
        return ((summed, counted), None)

    local_rows = fine_centroids.shape[0]
    start_state = (
        jnp.zeros(fine_centroids.shape, jnp.float32),
        jnp.zeros((local_rows,), jnp.float32),
    )
    stacked = (row_blocks, row_peak.reshape(-1, block_rows), row_mass.reshape(-1, block_rows))
    (fine_sums, fine_counts), _ = lax.scan(sum_step, start_state, stacked)
    total_sums, total_counts = lax.psum((fine_sums, fine_counts), "dp")
    pooled = fine_centroids + total_sums
    mass_rows = 1.0 + total_counts
    new_fine = pooled / mass_rows[:, None]
    col_width = feat_width // lax.axis_size("dp")
    first_col = lax.axis_index("dp") * col_width
    pooled_cols = lax.dynamic_slice_in_dim(pooled, first_col, col_width, 1)
    coarse_sum, coarse_mass = coarse_terms(parents, pooled_cols, mass_rows)
    owned_sum, owned_mass = (
        lax.psum_scatter(coarse_sum, "cent", scatter_dimension=0, tiled=True),
        lax.psum_scatter(coarse_mass, "cent", scatter_dimension=0, tiled=True),
    )
    old_cols = lax.dynamic_slice_in_dim(coarse_centroids, first_col, col_width, 1)
    new_cols = (coarse_prior * old_cols + owned_sum) / (coarse_prior + owned_mass)[:, None]
    new_coarse = lax.all_gather(new_cols, "dp", axis=1, tiled=True)
    return (new_fine, new_coarse)


def solution(mesh):
    in_specs = (P(("dp", "cent"), None), P("cent", None), P("cent"), P("cent", None))
    out_specs = (P("cent", None), P("cent", None))
    return jax.shard_map(local, mesh=mesh, in_specs=in_specs, out_specs=out_specs, check_vma=False)
```

profile of v0, /device:TPU:0, one launch (start us, length us, event | category | flops | bytes accessed | tf_op | source)
XLA Modules:
  0.0 365.4 jit_solution(11755867619514082077)
XLA Ops:
  7.2 0.0 all-gather.2.cloned.1.call-start
  7.2 0.7 all-gather.2.cloned.1.call-update
  7.9 0.0 all-reduce.3.cloned.1.call-start
  8.0 2.1 multiply_reduce_fusion
  10.1 71.3 %all-gather.2.cloned.1.call-done = bf16[2048,768]{1,0:T(8,128)(2,1)} async-done(((bf16[128,768]{1,0:T(8,128)(2,1)}), bf16[2048,768]{1,0:T(8,128)(2,1)}) %all-gather.2.cloned.1.call-update) | async-done | bytes 3145744 | tf_op jit(solution)/shard_map/all_gather | solution.py:26
  81.4 7.3 %while.33 = (s32[]{:T(128)}, f32[4,512]{1,0:T(4,128)S(1)}, bf16[4,512,768]{2,1,0:T(8,128)(2,1)}, bf16[512,768]{1,0:T(8,128)(2,1)S(1)}, f32[512]{0:T(512)S(1)}, /*index=5*/s32[]{:T(128)}, s32[]{:T(128)}) while((s32[]{:T(128)}, f32[4,512]{1,0:T(4,128)S(1)}, bf16[4,512,768]{2,1,0:T(8,128)(2,1)}, bf16[512,768]{1,0:T(8,128)(2,1)S(1)}, ...), condition=%wide.region_3.4_spmd, body=%wide.region_1.3_spmd.sunk | while | flops 403439104 | bytes 1581649 | solution.py:39
  81.4 1.7 fusion.44
  83.1 0.1 dynamic_update_slice.9
  83.2 1.8 fusion.44
  85.0 0.1 dynamic_update_slice.9
  85.0 1.8 fusion.44
  86.8 0.1 dynamic_update_slice.9
  86.8 1.8 fusion.44
  88.6 0.1 dynamic_update_slice.9
  88.7 39.8 %pmax.7 = f32[4,512]{1,0:T(4,128)S(1)} all-reduce(f32[4,512]{1,0:T(4,128)S(1)} %get-tuple-element.104), channel_id=1, replica_groups=mesh['dp'=2,'cent'=16] {'cent'}, use_global_device_ids=true, to_apply=%region_4.5 | all-reduce | flops 2048 | bytes 16384 | tf_op jit(solution)/shard_map/pmax | solution.py:40
  128.5 7.7 %while.34 = (s32[]{:T(128)}, f32[4,512]{1,0:T(4,128)S(1)}, bf16[4,512,768]{2,1,0:T(8,128)(2,1)}, bf16[512,768]{1,0:T(8,128)(2,1)S(1)}, f32[512]{0:T(512)S(1)}, /*index=5*/f32[4,512]{1,0:T(4,128)S(1)}, s32[]{:T(128)}, s32[]{:T(128)}) while((s32[]{:T(128)}, f32[4,512]{1,0:T(4,128)S(1)}, bf16[4,512,768]{2,1,0:T(8,128)(2,1)}, ...), condition=%wide.region_7.8_spmd, body=%wide.region_5.7_spmd.sunk | while | flops 403701248 | bytes 1587805 | solution.py:47
  128.5 1.8 fusion.47
  130.4 0.1 dynamic_update_slice.10
  130.5 1.8 fusion.47
  132.3 0.1 dynamic_update_slice.10
  132.4 1.8 fusion.47
  134.2 0.1 dynamic_update_slice.10
  134.3 1.8 fusion.47
  136.1 0.1 dynamic_update_slice.10
  136.2 37.1 %psum.21 = f32[4,512]{1,0:T(4,128)S(1)} all-reduce(f32[4,512]{1,0:T(4,128)S(1)} %get-tuple-element.105), channel_id=1, replica_groups=mesh['dp'=2,'cent'=16] {'cent'}, use_global_device_ids=true, to_apply=%region_8.9 | all-reduce | flops 2048 | bytes 16384 | tf_op jit(solution)/shard_map/psum | solution.py:48
  173.3 20.2 %while.35 = (s32[]{:T(128)}, f32[512,768]{1,0:T(8,128)S(1)}, f32[512]{0:T(512)S(1)}, bf16[4,512,768]{2,1,0:T(8,128)(2,1)}, bf16[512,768]{1,0:T(8,128)(2,1)S(1)},...) while((s32[]{:T(128)}, f32[512,768]{1,0:T(8,128)S(1)}, ...), condition=%wide.region_11.12_spmd.clone, body=%wide.region_9.11_spmd.clone.sunk | while | flops 2820669952 | bytes 7625844 | solution.py:71
  173.4 1.9 fusion.51
  175.2 3.1 select_add_fusion.4
  178.4 1.9 fusion.51
  180.3 3.1 select_add_fusion.4
  183.5 1.9 fusion.51
  185.4 3.1 select_add_fusion.4
  188.6 1.9 fusion.51
  190.4 3.1 select_add_fusion.4
  193.6 0.0 copy-start
  193.6 0.0 copy-start.1
  193.6 1.1 copy-done
  194.7 0.0 all-reduce.3.cloned.1.call-update
  194.8 0.0 reduce-scatter.2.cloned.1.call-start
  194.8 2.5 psum.23
  197.3 15.7 %all-reduce.3.cloned.1.call-done = f32[512,768]{1,0:T(8,128)} async-done(((f32[512,768]{1,0:T(8,128)}), f32[512,768]{1,0:T(8,128)}) %all-reduce.3.cloned.1.call-update) | async-done | bytes 1572880 | tf_op jit(solution)/shard_map/psum | solution.py:72
  213.0 0.0 copy-done.1
  213.0 2.8 broadcast_divide_fusion
  215.8 5.6 %scatter_custom_fusion = f32[2048,384]{1,0:T(8,128)} fusion(s32[512]{0:T(512)} %param.12, f32[]{:T(128)} %constant.35.clone.1, f32[512,768]{1,0:T(8,128)S(1)} %get-tuple-element.174, s32[]{:T(128)} %constant.39.clone.1, s32[]{:T(128)S(6)} %select_n.4), kind=kCustom, calls=%fused_computation.32 | custom fusion | flops 196608 | bytes 3933188 | tf_op jit(solution)/shard_map/scatter-add | solution.py:20
  221.4 0.0 copy-start.3
  221.4 0.0 copy-start.2
  221.4 0.0 reduce-scatter.2.cloned.1.call-update
  221.4 0.6 copy-done.3
  222.0 0.6 dynamic-slice
  223.3 3.4 scatter_custom_fusion.1
  226.7 42.6 %all-reduce = f32[2048]{0:T(1024)S(1)} all-reduce(f32[2048]{0:T(1024)S(1)} %scatter_custom_fusion.1), channel_id=3, replica_groups=mesh['dp'=2,'cent'=16] {'cent'}, use_global_device_ids=true, to_apply=%region_17.18.clone | all-reduce | flops 2048 | bytes 16384
  269.3 0.1 dynamic-slice_add_fusion
  269.4 85.6 %reduce-scatter.2.cloned.1.call-done = f32[128,384]{1,0:T(8,128)} async-done(((f32[2048,384]{1,0:T(8,128)}), f32[128,384]{1,0:T(8,128)}) %reduce-scatter.2.cloned.1.call-update) | async-done | bytes 196624 | tf_op jit(solution)/shard_map/reduce_scatter | solution.py:81
  355.0 0.0 copy-done.2
  355.0 1.0 add_divide_fusion
  356.0 2.1 all_gather.7
  358.1 0.7 copy.33
  (18 shorter events, 0.1 us)
Async XLA Ops:
  7.2 74.2 %all-gather.2.cloned.1.call-start = ((), (), s32[]{:S(2)}) async-start(), calls=%async_computation.1 | async-start | bytes 3342336 | tf_op jit(solution)/shard_map/all_gather | solution.py:26
  7.9 205.1 %all-reduce.3.cloned.1.call-start = ((), (), s32[]{:S(2)}) async-start(), calls=%async_computation.2 | async-start | bytes 3145728 | tf_op jit(solution)/shard_map/psum | solution.py:72
  193.6 1.1 copy-start
  193.6 19.4 %copy-start.1 = (f32[512,768]{1,0:T(8,128)S(1)}, f32[512,768]{1,0:T(8,128)}, u32[]{:S(2)}) copy-start(f32[512,768]{1,0:T(8,128)} %param.11) | copy-start | bytes 4718596
  194.8 160.3 %reduce-scatter.2.cloned.1.call-start = ((), (), s32[]{:S(2)}) async-start(), calls=%async_computation.3 | async-start | bytes 3342336 | tf_op jit(solution)/shard_map/reduce_scatter | solution.py:81
  221.4 0.7 copy-start.3
  221.4 133.6 %copy-start.2 = (f32[128,768]{1,0:T(8,128)S(1)}, f32[128,768]{1,0:T(8,128)}, u32[]{:S(2)}) copy-start(f32[128,768]{1,0:T(8,128)} %param.13) | copy-start | bytes 1179652
Sparse Core Ops, SparseCore 0:
  10.7 70.5 all-gather.1
  194.9 18.0 all-reduce.2
  221.5 133.4 reduce-scatter.1
where the time goes:
time: 366 us; the launch traced here: 365 us
  waiting for transfers between devices  173 us (47%)
  blocking collectives  124 us (34%)
  matrix products  34.3 us (9%)
  other arithmetic  15.1 us (4%)
  between operations  14.5 us (4%)
    reduce_scatter x1, waiting for transfers between devices, local(): lax.psum_scatter(coarse_sum, 'cent', scatter_dimension=0, tiled=True)  85.6 us
    all_gather x1, waiting for transfers between devices, local(): gathered = lax.all_gather(embeddings, 'cent', axis=0, tiled=True)  71.3 us
    unnamed x1, blocking collectives  42.6 us
    pmax x1, blocking collectives, local(): row_peak = lax.pmax(local_peak.reshape(-1), 'cent')  39.8 us
    psum x1, blocking collectives, local(): row_mass = lax.psum(local_mass.reshape(-1), 'cent')  37.1 us
    dot_general x12, matrix products, block_logits(): lax.dot_general(one_block, narrow_centroids, (((1,), (1,)), ((), ())), pr...  21.8 us
    psum x1, waiting for transfers between devices, local(): total_sums, total_counts = lax.psum((fine_sums, fine_counts), 'dp')  15.7 us
    dot_general x4, matrix products, sum_step(): lax.dot_general(soft_weights, wide_block, (((0,), (0,)), ((), ())), preci...  12.5 us
  transfers between devices with their start and end apart: 3, of which 3 were waited for; matrix products, arithmetic and copies ran while one was open for 2% of the time, Pallas kernels for 0%

commit v1 on v0

--- a/solution.py
+++ b/solution.py
@@ -23,7 +23,12 @@
 
 
 def local(embeddings, fine_centroids, parents, coarse_centroids):
-    gathered = lax.all_gather(embeddings, "cent", axis=0, tiled=True)
+    ring = [embeddings]
+    for hop in range(15):
+        ring.append(lax.ppermute(ring[-1], "cent", [(dev, (dev + 1) % 16) for dev in range(16)]))
+    gathered = jnp.roll(
+        jnp.concatenate(ring[::-1], axis=0), (lax.axis_index("cent") + 1) * ring[0].shape[0], axis=0
+    )
     row_count = gathered.shape[0]
     feat_width = gathered.shape[1]
     block_rows = math.gcd(row_count, 512)

time: 366 us -> 451 us (1.23)
  waiting for transfers between devices: 173 us -> 242 us
  local copies, waits for them, and re-layouts: 3.56 us -> 12.2 us
    ppermute x0 -> x15, waiting for transfers between devices: none -> 142 us  [local(): lax.ppermute(ring[-1], 'cent', [(dev, (dev + 1) % 16) for dev in range(16)])]
    all_gather x1 -> x0, waiting for transfers between devices: 71.3 us -> none  [local(): gathered = lax.all_gather(embeddings, 'cent', axis=0, tiled=True)]
    unnamed x10 -> x49, local copies, waits for them, and re-layouts: 3.09 us -> 9.87 us
  transfers between devices with their start and end apart: 3 -> 17, of which waited for: 3 -> 17; matrix products, arithmetic and copies ran while one was open for 2% -> 2% of each run, Pallas kernels for 0% -> 0%
where the time goes in v1:
time: 451 us; the launch traced here: 450 us
  waiting for transfers between devices  242 us (54%)
  blocking collectives  123 us (27%)
  matrix products  37.2 us (8%)
  other arithmetic  16.4 us (4%)
  between operations  15.1 us (3%)
  local copies, waits for them, and re-layouts  12.2 us (3%)
    ppermute x15, waiting for transfers between devices, local(): lax.ppermute(ring[-1], 'cent', [(dev, (dev + 1) % 16) for dev in range(16)])  142 us
    reduce_scatter x1, waiting for transfers between devices, local(): lax.psum_scatter(coarse_sum, 'cent', scatter_dimension=0, tiled=True)  86.2 us
    unnamed x1, blocking collectives  42.8 us
    psum x1, blocking collectives, local(): row_mass = lax.psum(local_mass.reshape(-1), 'cent')  39.1 us
    pmax x1, blocking collectives, local(): row_peak = lax.pmax(local_peak.reshape(-1), 'cent')  37.1 us
    dot_general x12, matrix products, block_logits(): lax.dot_general(one_block, narrow_centroids, (((1,), (1,)), ((), ())), pr...  24.7 us
    psum x1, waiting for transfers between devices, local(): total_sums, total_counts = lax.psum((fine_sums, fine_counts), 'dp')  13.8 us
    dot_general x4, matrix products, sum_step(): lax.dot_general(soft_weights, wide_block, (((0,), (0,)), ((), ())), preci...  12.5 us
  transfers between devices with their start and end apart: 17, of which 17 were waited for; matrix products, arithmetic and copies ran while one was open for 2% of the time, Pallas kernels for 0%

profile of v1, /device:TPU:0, one launch (start us, length us, event | category | flops | bytes accessed | tf_op | source)
XLA Modules:
  0.0 449.7 jit_solution(14679435636124609121)
XLA Ops:
  7.2 3.0 collective-permute-start
  10.2 9.1 %collective-permute-done = bf16[128,768]{1,0:T(8,128)(2,1)S(1)} collective-permute-done((bf16[128,768]{1,0:T(8,128)(2,1)}, bf16[128,768]{1,0:T(8,128)(2,1)S(1)}, u32[]{:S(2)}, u32[]{:S(2)}) %collective-permute-start) | collective-permute-done | bytes 196640 | tf_op jit(solution)/shard_map/ppermute | solution.py:28
  19.3 9.7 %collective-permute-done.1 = bf16[128,768]{1,0:T(8,128)(2,1)S(1)} collective-permute-done((bf16[128,768]{1,0:T(8,128)(2,1)S(1)}, bf16[128,768]{1,0:T(8,128)(2,1)S(1)}, u32[]{:S(2)}, u32[]{:S(2)}) %collective-permute-start.1) | collective-permute-done | bytes 196640 | tf_op jit(solution)/shard_map/ppermute | solution.py:28
  29.0 9.3 %collective-permute-done.2 = bf16[128,768]{1,0:T(8,128)(2,1)S(1)} collective-permute-done((bf16[128,768]{1,0:T(8,128)(2,1)S(1)}, bf16[128,768]{1,0:T(8,128)(2,1)S(1)}, u32[]{:S(2)}, u32[]{:S(2)}) %collective-permute-start.2) | collective-permute-done | bytes 196640 | tf_op jit(solution)/shard_map/ppermute | solution.py:28
  38.3 9.3 %collective-permute-done.3 = bf16[128,768]{1,0:T(8,128)(2,1)S(1)} collective-permute-done((bf16[128,768]{1,0:T(8,128)(2,1)S(1)}, bf16[128,768]{1,0:T(8,128)(2,1)S(1)}, u32[]{:S(2)}, u32[]{:S(2)}) %collective-permute-start.3) | collective-permute-done | bytes 196640 | tf_op jit(solution)/shard_map/ppermute | solution.py:28
  47.5 9.3 %collective-permute-done.4 = bf16[128,768]{1,0:T(8,128)(2,1)S(1)} collective-permute-done((bf16[128,768]{1,0:T(8,128)(2,1)S(1)}, bf16[128,768]{1,0:T(8,128)(2,1)S(1)}, u32[]{:S(2)}, u32[]{:S(2)}) %collective-permute-start.4) | collective-permute-done | bytes 196640 | tf_op jit(solution)/shard_map/ppermute | solution.py:28
  56.8 9.3 %collective-permute-done.5 = bf16[128,768]{1,0:T(8,128)(2,1)S(1)} collective-permute-done((bf16[128,768]{1,0:T(8,128)(2,1)S(1)}, bf16[128,768]{1,0:T(8,128)(2,1)S(1)}, u32[]{:S(2)}, u32[]{:S(2)}) %collective-permute-start.5) | collective-permute-done | bytes 196640 | tf_op jit(solution)/shard_map/ppermute | solution.py:28
  66.1 10.4 %collective-permute-done.6 = bf16[128,768]{1,0:T(8,128)(2,1)S(1)} collective-permute-done((bf16[128,768]{1,0:T(8,128)(2,1)S(1)}, bf16[128,768]{1,0:T(8,128)(2,1)S(1)}, u32[]{:S(2)}, u32[]{:S(2)}) %collective-permute-start.6) | collective-permute-done | bytes 196640 | tf_op jit(solution)/shard_map/ppermute | solution.py:28
  76.5 11.2 %collective-permute-done.7 = bf16[128,768]{1,0:T(8,128)(2,1)S(1)} collective-permute-done((bf16[128,768]{1,0:T(8,128)(2,1)S(1)}, bf16[128,768]{1,0:T(8,128)(2,1)S(1)}, u32[]{:S(2)}, u32[]{:S(2)}) %collective-permute-start.7) | collective-permute-done | bytes 196640 | tf_op jit(solution)/shard_map/ppermute | solution.py:28
  87.7 10.3 %collective-permute-done.8 = bf16[128,768]{1,0:T(8,128)(2,1)S(1)} collective-permute-done((bf16[128,768]{1,0:T(8,128)(2,1)S(1)}, bf16[128,768]{1,0:T(8,128)(2,1)S(1)}, u32[]{:S(2)}, u32[]{:S(2)}) %collective-permute-start.8) | collective-permute-done | bytes 196640 | tf_op jit(solution)/shard_map/ppermute | solution.py:28
  98.0 10.1 %collective-permute-done.9 = bf16[128,768]{1,0:T(8,128)(2,1)S(1)} collective-permute-done((bf16[128,768]{1,0:T(8,128)(2,1)S(1)}, bf16[128,768]{1,0:T(8,128)(2,1)S(1)}, u32[]{:S(2)}, u32[]{:S(2)}) %collective-permute-start.9) | collective-permute-done | bytes 196640 | tf_op jit(solution)/shard_map/ppermute | solution.py:28
  108.1 0.7 copy-done.2
  108.8 9.3 %collective-permute-done.10 = bf16[128,768]{1,0:T(8,128)(2,1)S(1)} collective-permute-done((bf16[128,768]{1,0:T(8,128)(2,1)S(1)}, bf16[128,768]{1,0:T(8,128)(2,1)S(1)}, u32[]{:S(2)}, u32[]{:S(2)}) %collective-permute-start.10) | collective-permute-done | bytes 196640 | tf_op jit(solution)/shard_map/ppermute | solution.py:28
  118.1 0.7 copy-done.4
  118.8 9.4 %collective-permute-done.11 = bf16[128,768]{1,0:T(8,128)(2,1)} collective-permute-done((bf16[128,768]{1,0:T(8,128)(2,1)S(1)}, bf16[128,768]{1,0:T(8,128)(2,1)}, u32[]{:S(2)}, u32[]{:S(2)}) %collective-permute-start.11) | collective-permute-done | bytes 196640 | tf_op jit(solution)/shard_map/ppermute | solution.py:28
  128.2 9.6 %collective-permute-done.12 = bf16[128,768]{1,0:T(8,128)(2,1)} collective-permute-done((bf16[128,768]{1,0:T(8,128)(2,1)}, bf16[128,768]{1,0:T(8,128)(2,1)}, u32[]{:S(2)}, u32[]{:S(2)}) %collective-permute-start.12) | collective-permute-done | bytes 196640 | tf_op jit(solution)/shard_map/ppermute | solution.py:28
  137.7 2.9 multiply_reduce_fusion
  140.7 6.5 %collective-permute-done.13 = bf16[128,768]{1,0:T(8,128)(2,1)S(1)} collective-permute-done((bf16[128,768]{1,0:T(8,128)(2,1)}, bf16[128,768]{1,0:T(8,128)(2,1)S(1)}, u32[]{:S(2)}, u32[]{:S(2)}) %collective-permute-start.13) | collective-permute-done | bytes 196640 | tf_op jit(solution)/shard_map/ppermute | solution.py:28
  147.2 9.3 %collective-permute-done.14 = bf16[128,768]{1,0:T(8,128)(2,1)S(1)} collective-permute-done((bf16[128,768]{1,0:T(8,128)(2,1)S(1)}, bf16[128,768]{1,0:T(8,128)(2,1)S(1)}, u32[]{:S(2)}, u32[]{:S(2)}) %collective-permute-start.14) | collective-permute-done | bytes 196640 | tf_op jit(solution)/shard_map/ppermute | solution.py:28
  156.5 0.9 constant_dynamic-update-slice_fusion.29
  157.5 0.9 constant_dynamic-update-slice_fusion.28
  158.4 0.9 constant_dynamic-update-slice_fusion.27
  159.3 0.9 constant_dynamic-update-slice_fusion.26
  160.6 0.9 constant_dynamic-update-slice_fusion.13
  161.5 0.9 constant_dynamic-update-slice_fusion.12
  162.8 1.9 constant_dynamic-slice_fusion.3
  164.6 8.2 %while.33 = (s32[]{:T(128)}, f32[4,512]{1,0:T(4,128)S(1)}, bf16[4,512,768]{2,1,0:T(8,128)(2,1)}, bf16[512,768]{1,0:T(8,128)(2,1)}, f32[512]{0:T(512)S(1)}, /*index=5*/s32[]{:T(128)}, s32[]{:T(128)}) while((s32[]{:T(128)}, f32[4,512]{1,0:T(4,128)S(1)}, bf16[4,512,768]{2,1,0:T(8,128)(2,1)}, bf16[512,768]{1,0:T(8,128)(2,1)}, f32[512]{0:T(512)S(1)}, ...), condition=%wide.region_3.4_spmd, body=%wide.region_1.3_spmd.sunk | while | flops 403439104 | bytes 1581649 | solution.py:44
  164.6 2.0 fusion.44
  166.6 0.1 dynamic_update_slice.9
  166.7 2.0 fusion.44
  168.7 0.1 dynamic_update_slice.9
  168.8 2.0 fusion.44
  170.8 0.1 dynamic_update_slice.9
  170.8 2.0 fusion.44
  172.8 0.1 dynamic_update_slice.9
  172.9 37.1 %pmax.7 = f32[4,512]{1,0:T(4,128)S(1)} all-reduce(f32[4,512]{1,0:T(4,128)S(1)} %get-tuple-element.104), channel_id=1, replica_groups=mesh['dp'=2,'cent'=16] {'cent'}, use_global_device_ids=true, to_apply=%region_4.5 | all-reduce | flops 2048 | bytes 16384 | tf_op jit(solution)/shard_map/pmax | solution.py:45
  210.0 8.6 %while.34 = (s32[]{:T(128)}, f32[4,512]{1,0:T(4,128)S(1)}, bf16[4,512,768]{2,1,0:T(8,128)(2,1)}, bf16[512,768]{1,0:T(8,128)(2,1)}, f32[512]{0:T(512)S(1)}, /*index=5*/f32[4,512]{1,0:T(4,128)S(1)}, s32[]{:T(128)}, s32[]{:T(128)}) while((s32[]{:T(128)}, f32[4,512]{1,0:T(4,128)S(1)}, bf16[4,512,768]{2,1,0:T(8,128)(2,1)}, ...), condition=%wide.region_7.8_spmd, body=%wide.region_5.7_spmd.sunk | while | flops 403701248 | bytes 1587805 | solution.py:52
  210.0 2.1 fusion.47
  212.2 2.1 fusion.47
  214.3 2.1 fusion.47
  216.5 2.1 fusion.47
  218.6 39.1 %psum.21 = f32[4,512]{1,0:T(4,128)S(1)} all-reduce(f32[4,512]{1,0:T(4,128)S(1)} %get-tuple-element.105), channel_id=1, replica_groups=mesh['dp'=2,'cent'=16] {'cent'}, use_global_device_ids=true, to_apply=%region_8.9 | all-reduce | flops 2048 | bytes 16384 | tf_op jit(solution)/shard_map/psum | solution.py:53
  257.7 21.2 %while.35 = (s32[]{:T(128)}, f32[512,768]{1,0:T(8,128)S(1)}, f32[512]{0:T(512)S(1)}, bf16[4,512,768]{2,1,0:T(8,128)(2,1)}, bf16[512,768]{1,0:T(8,128)(2,1)}, /*i...) while((s32[]{:T(128)}, f32[512,768]{1,0:T(8,128)S(1)}, ...), condition=%wide.region_11.12_spmd.clone, body=%wide.region_9.11_spmd.clone.sunk | while | flops 2820669952 | bytes 7625844 | solution.py:76
  257.7 2.1 fusion.51
  259.8 3.1 select_add_fusion.4
  263.0 2.1 fusion.51
  265.1 3.1 select_add_fusion.4
  268.3 2.1 fusion.51
  270.4 3.1 select_add_fusion.4
  273.6 2.1 fusion.51
  275.7 3.1 select_add_fusion.4
  278.9 1.1 copy-done
  280.1 2.5 psum.23
  282.6 13.8 %all-reduce.3.cloned.1.call-done = f32[512,768]{1,0:T(8,128)} async-done(((f32[512,768]{1,0:T(8,128)}), f32[512,768]{1,0:T(8,128)}) %all-reduce.3.cloned.1.call-update) | async-done | bytes 1572880 | tf_op jit(solution)/shard_map/psum | solution.py:77
  296.4 3.3 broadcast_divide_fusion
  299.7 5.6 %scatter_custom_fusion = f32[2048,384]{1,0:T(8,128)} fusion(s32[512]{0:T(512)} %param.12, f32[]{:T(128)} %constant.78.clone.1, f32[512,768]{1,0:T(8,128)S(1)} %get-tuple-element.174, s32[]{:T(128)} %constant.77.clone.1, s32[]{:T(128)S(6)} %select_n.19), kind=kCustom, calls=%fused_computation.32 | custom fusion | flops 196608 | bytes 3933188 | tf_op jit(solution)/shard_map/scatter-add | solution.py:20
  305.3 0.6 dynamic-slice
  306.6 3.4 scatter_custom_fusion.1
  310.0 42.8 %all-reduce = f32[2048]{0:T(1024)S(1)} all-reduce(f32[2048]{0:T(1024)S(1)} %scatter_custom_fusion.1), channel_id=3, replica_groups=mesh['dp'=2,'cent'=16] {'cent'}, use_global_device_ids=true, to_apply=%region_17.18.clone | all-reduce | flops 2048 | bytes 16384
  352.7 0.1 dynamic-slice_add_fusion
  352.8 86.2 %reduce-scatter.2.cloned.1.call-done = f32[128,384]{1,0:T(8,128)} async-done(((f32[2048,384]{1,0:T(8,128)}), f32[128,384]{1,0:T(8,128)}) %reduce-scatter.2.cloned.1.call-update) | async-done | bytes 196624 | tf_op jit(solution)/shard_map/reduce_scatter | solution.py:86
  439.0 1.0 add_divide_fusion
  440.1 2.1 all_gather.3
  442.1 0.7 copy.64
  (79 shorter events, 0.9 us)
Async XLA Ops:
  7.2 153.3 %copy-start.1 = (bf16[128,768]{1,0:T(8,128)(2,1)S(1)}, bf16[128,768]{1,0:T(8,128)(2,1)}, u32[]{:S(2)}) copy-start(bf16[128,768]{1,0:T(8,128)(2,1)} %param.10) | copy-start | bytes 589828
  7.2 289.3 %all-reduce.3.cloned.1.call-start = ((), (), s32[]{:S(2)}) async-start(), calls=%async_computation.1 | async-start | bytes 3145728 | tf_op jit(solution)/shard_map/psum | solution.py:77
  7.2 12.1 %collective-permute-start = (bf16[128,768]{1,0:T(8,128)(2,1)}, bf16[128,768]{1,0:T(8,128)(2,1)S(1)}, u32[]{:S(2)}, u32[]{:S(2)}) collective-permute-start(bf16[128,768]{1,0:T(8,128)(2,1)} %param.10), channel_id=1, source_target_pairs={{0,1},{1,2},{2,3},{3,4},{4,5},{5,6},{6,7},{7,8},{8,9},{9,10},{10,1... | collective-permute-start | bytes 589832 | tf_op jit(solution)/shard_map/ppermute | solution.py:28
  19.3 9.7 %collective-permute-start.1 = (bf16[128,768]{1,0:T(8,128)(2,1)S(1)}, bf16[128,768]{1,0:T(8,128)(2,1)S(1)}, u32[]{:S(2)}, u32[]{:S(2)}) collective-permute-start(bf16[128,768]{1,0:T(8,128)(2,1)S(1)} %collective-permute-done), channel_id=1, source_target_pairs={{0,1},{1,2},{2,3},{3,4},{4,5},{5,6},{6,7},{7,8},{8,9},{9,10},{10,1... | collective-permute-start | bytes 589832 | tf_op jit(solution)/shard_map/ppermute | solution.py:28
  29.0 9.3 %collective-permute-start.2 = (bf16[128,768]{1,0:T(8,128)(2,1)S(1)}, bf16[128,768]{1,0:T(8,128)(2,1)S(1)}, u32[]{:S(2)}, u32[]{:S(2)}) collective-permute-start(bf16[128,768]{1,0:T(8,128)(2,1)S(1)} %collective-permute-done.1), channel_id=1, source_target_pairs={{0,1},{1,2},{2,3},{3,4},{4,5},{5,6},{6,7},{7,8},{8,9},{9,10},{10,1... | collective-permute-start | bytes 589832 | tf_op jit(solution)/shard_map/ppermute | solution.py:28
  38.3 9.3 %collective-permute-start.3 = (bf16[128,768]{1,0:T(8,128)(2,1)S(1)}, bf16[128,768]{1,0:T(8,128)(2,1)S(1)}, u32[]{:S(2)}, u32[]{:S(2)}) collective-permute-start(bf16[128,768]{1,0:T(8,128)(2,1)S(1)} %collective-permute-done.2), channel_id=1, source_target_pairs={{0,1},{1,2},{2,3},{3,4},{4,5},{5,6},{6,7},{7,8},{8,9},{9,10},{10,1... | collective-permute-start | bytes 589832 | tf_op jit(solution)/shard_map/ppermute | solution.py:28
  47.5 9.3 %collective-permute-start.4 = (bf16[128,768]{1,0:T(8,128)(2,1)S(1)}, bf16[128,768]{1,0:T(8,128)(2,1)S(1)}, u32[]{:S(2)}, u32[]{:S(2)}) collective-permute-start(bf16[128,768]{1,0:T(8,128)(2,1)S(1)} %collective-permute-done.3), channel_id=1, source_target_pairs={{0,1},{1,2},{2,3},{3,4},{4,5},{5,6},{6,7},{7,8},{8,9},{9,10},{10,1... | collective-permute-start | bytes 589832 | tf_op jit(solution)/shard_map/ppermute | solution.py:28
  56.8 9.3 %collective-permute-start.5 = (bf16[128,768]{1,0:T(8,128)(2,1)S(1)}, bf16[128,768]{1,0:T(8,128)(2,1)S(1)}, u32[]{:S(2)}, u32[]{:S(2)}) collective-permute-start(bf16[128,768]{1,0:T(8,128)(2,1)S(1)} %collective-permute-done.4), channel_id=1, source_target_pairs={{0,1},{1,2},{2,3},{3,4},{4,5},{5,6},{6,7},{7,8},{8,9},{9,10},{10,1... | collective-permute-start | bytes 589832 | tf_op jit(solution)/shard_map/ppermute | solution.py:28
  66.1 10.4 %collective-permute-start.6 = (bf16[128,768]{1,0:T(8,128)(2,1)S(1)}, bf16[128,768]{1,0:T(8,128)(2,1)S(1)}, u32[]{:S(2)}, u32[]{:S(2)}) collective-permute-start(bf16[128,768]{1,0:T(8,128)(2,1)S(1)} %collective-permute-done.5), channel_id=1, source_target_pairs={{0,1},{1,2},{2,3},{3,4},{4,5},{5,6},{6,7},{7,8},{8,9},{9,10},{10,1... | collective-permute-start | bytes 589832 | tf_op jit(solution)/shard_map/ppermute | solution.py:28
  76.5 11.2 %collective-permute-start.7 = (bf16[128,768]{1,0:T(8,128)(2,1)S(1)}, bf16[128,768]{1,0:T(8,128)(2,1)S(1)}, u32[]{:S(2)}, u32[]{:S(2)}) collective-permute-start(bf16[128,768]{1,0:T(8,128)(2,1)S(1)} %collective-permute-done.6), channel_id=1, source_target_pairs={{0,1},{1,2},{2,3},{3,4},{4,5},{5,6},{6,7},{7,8},{8,9},{9,10},{10,1... | collective-permute-start | bytes 589832 | tf_op jit(solution)/shard_map/ppermute | solution.py:28
  87.7 10.3 %collective-permute-start.8 = (bf16[128,768]{1,0:T(8,128)(2,1)S(1)}, bf16[128,768]{1,0:T(8,128)(2,1)S(1)}, u32[]{:S(2)}, u32[]{:S(2)}) collective-permute-start(bf16[128,768]{1,0:T(8,128)(2,1)S(1)} %collective-permute-done.7), channel_id=1, source_target_pairs={{0,1},{1,2},{2,3},{3,4},{4,5},{5,6},{6,7},{7,8},{8,9},{9,10},{10,1... | collective-permute-start | bytes 589832 | tf_op jit(solution)/shard_map/ppermute | solution.py:28
  98.0 10.1 %collective-permute-start.9 = (bf16[128,768]{1,0:T(8,128)(2,1)S(1)}, bf16[128,768]{1,0:T(8,128)(2,1)S(1)}, u32[]{:S(2)}, u32[]{:S(2)}) collective-permute-start(bf16[128,768]{1,0:T(8,128)(2,1)S(1)} %collective-permute-done.8), channel_id=1, source_target_pairs={{0,1},{1,2},{2,3},{3,4},{4,5},{5,6},{6,7},{7,8},{8,9},{9,10},{10,1... | collective-permute-start | bytes 589832 | tf_op jit(solution)/shard_map/ppermute | solution.py:28
  108.1 0.7 copy-start.2
  108.8 9.3 %collective-permute-start.10 = (bf16[128,768]{1,0:T(8,128)(2,1)S(1)}, bf16[128,768]{1,0:T(8,128)(2,1)S(1)}, u32[]{:S(2)}, u32[]{:S(2)}) collective-permute-start(bf16[128,768]{1,0:T(8,128)(2,1)S(1)} %collective-permute-done.9), channel_id=1, source_target_pairs={{0,1},{1,2},{2,3},{3,4},{4,5},{5,6},{6,7},{7,8},{8,9},{9,10},{10,1... | collective-permute-start | bytes 589832 | tf_op jit(solution)/shard_map/ppermute | solution.py:28
  118.1 0.7 copy-start.4
  118.8 9.4 %collective-permute-start.11 = (bf16[128,768]{1,0:T(8,128)(2,1)S(1)}, bf16[128,768]{1,0:T(8,128)(2,1)}, u32[]{:S(2)}, u32[]{:S(2)}) collective-permute-start(bf16[128,768]{1,0:T(8,128)(2,1)S(1)} %collective-permute-done.10), channel_id=1, source_target_pairs={{0,1},{1,2},{2,3},{3,4},{4,5},{5,6},{6,7},{7,8},{8,9},{9,10},{10,1... | collective-permute-start | bytes 589832 | tf_op jit(solution)/shard_map/ppermute | solution.py:28
  128.1 9.6 %collective-permute-start.12 = (bf16[128,768]{1,0:T(8,128)(2,1)}, bf16[128,768]{1,0:T(8,128)(2,1)}, u32[]{:S(2)}, u32[]{:S(2)}) collective-permute-start(bf16[128,768]{1,0:T(8,128)(2,1)} %collective-permute-done.11), channel_id=1, source_target_pairs={{0,1},{1,2},{2,3},{3,4},{4,5},{5,6},{6,7},{7,8},{8,9},{9,10},{10,1... | collective-permute-start | bytes 589832 | tf_op jit(solution)/shard_map/ppermute | solution.py:28
  128.2 34.3 %copy-start.5 = (bf16[128,768]{1,0:T(8,128)(2,1)S(1)}, bf16[128,768]{1,0:T(8,128)(2,1)}, u32[]{:S(2)}) copy-start(bf16[128,768]{1,0:T(8,128)(2,1)} %copy-done.4) | copy-start | bytes 589828
  128.2 34.4 %copy-start.3 = (bf16[128,768]{1,0:T(8,128)(2,1)S(1)}, bf16[128,768]{1,0:T(8,128)(2,1)}, u32[]{:S(2)}) copy-start(bf16[128,768]{1,0:T(8,128)(2,1)} %copy-done.2) | copy-start | bytes 589828
  137.7 9.5 %collective-permute-start.13 = (bf16[128,768]{1,0:T(8,128)(2,1)}, bf16[128,768]{1,0:T(8,128)(2,1)S(1)}, u32[]{:S(2)}, u32[]{:S(2)}) collective-permute-start(bf16[128,768]{1,0:T(8,128)(2,1)} %collective-permute-done.12), channel_id=1, source_target_pairs={{0,1},{1,2},{2,3},{3,4},{4,5},{5,6},{6,7},{7,8},{8,9},{9,10},{10,1... | collective-permute-start | bytes 589832 | tf_op jit(solution)/shard_map/ppermute | solution.py:28
  147.2 9.3 %collective-permute-start.14 = (bf16[128,768]{1,0:T(8,128)(2,1)S(1)}, bf16[128,768]{1,0:T(8,128)(2,1)S(1)}, u32[]{:S(2)}, u32[]{:S(2)}) collective-permute-start(bf16[128,768]{1,0:T(8,128)(2,1)S(1)} %collective-permute-done.13), channel_id=1, source_target_pairs={{0,1},{1,2},{2,3},{3,4},{4,5},{5,6},{6,7},{7,8},{8,9},{9,10},{10,1... | collective-permute-start | bytes 589832 | tf_op jit(solution)/shard_map/ppermute | solution.py:28
  278.9 1.1 copy-start
  280.1 159.0 %reduce-scatter.2.cloned.1.call-start = ((), (), s32[]{:S(2)}) async-start(), calls=%async_computation.2 | async-start | bytes 3342336 | tf_op jit(solution)/shard_map/reduce_scatter | solution.py:86
  282.6 22.7 %copy-start.7 = (u32[32]{0:T(128)S(1)}, u32[32]{0:T(128)}, u32[]{:S(2)}) copy-start(u32[32]{0:T(128)} %constant.94) | copy-start | bytes 388
  282.6 156.4 %copy-start.6 = (f32[128,768]{1,0:T(8,128)S(1)}, f32[128,768]{1,0:T(8,128)}, u32[]{:S(2)}) copy-start(f32[128,768]{1,0:T(8,128)} %param.13) | copy-start | bytes 1179652
Sparse Core Ops, SparseCore 0:
  280.2 16.2 all-reduce.2
  305.4 133.5 reduce-scatter.1
